TPU v7x, 32 devices: a whole 2x2x4 slice. The times are simulated.
32 devices in a mesh: samp: 8 (over z, core), chan: 4 (over y, x).
Axes of the slice: x: 2, y: 2, z: 4, core: 2. Of those that a mesh axis runs over, the one named last changes fastest.
Arguments:
- out_cot: bfloat16 [8, 256, 4096], P('samp', 'chan'), may hold values from -6 to 6
- mix_weight: bfloat16 [256, 256], replicated, may hold values from -0.375 to 0.375
- corr_kernels: float32 [2, 12, 256, 64], P(None, None, 'chan'), may hold values from -0.75 to 0.75
- momentum: int32 [8], P('samp'), may hold values from 0 to 11
- spin_up: int32 [8, 4096], P('samp', 'chan'), may hold values 0 or 1
- layer_input: bfloat16 [8, 256, 4096], P('samp', None, 'chan'), may hold values from -6 to 6
- pre_one: bfloat16 [8, 256, 4096], P('samp', None, 'chan'), may hold values from -6 to 6
- pre_two: bfloat16 [8, 256, 4096], P('samp', None, 'chan'), may hold values from -6 to 6
- conv_weight: bfloat16 [3, 9, 256, 256], replicated, may hold values from -0.125 to 0.125
- dilation: int32 [3, 256], replicated, may hold values from 1 to 4, as said below
Outputs:
- input_grad: bfloat16 [8, 256, 4096], P('samp', None, 'chan')
- weight_grad: float32 [3, 9, 256, 256], P(None, None, 'chan')
Inputs may be any that keep to these rules, and one draw needn't show every extreme that they name: Some channel of every convolution has dilation 4.
All inputs are finite; a program needn't handle non-finite values. No bound on the sum of `spin_up` on one device may be relied on, other than what follows from the above.
Results may differ from a plain program's by a relative error of at most 0.02.
Values may be sent and summed in bfloat16 or wider, within the bound.
A program may use at most 64 MiB of HBM per device.

v0:
```python
import math
import jax
import jax.numpy as jnp
from jax import lax
from jax.sharding import PartitionSpec as P

SIDE = 64
LAYERS = 3
MAXDIL = 4


def with_halo(shard, sides, width):
    for axis, dim in sides:
        size, length = (lax.axis_size(axis), shard.shape[dim])
        up = [(i, (i + 1) % size) for i in range(size)]
        down = [(j, i) for i, j in up]
        last = lax.slice_in_dim(shard, length - width, length, axis=dim)
        leading = lax.slice_in_dim(shard, 0, width, axis=dim)
        before = lax.ppermute(last, axis, up)
        after = lax.ppermute(leading, axis, down)
        shard = jnp.concatenate([before, shard, after], axis=dim)
    return shard


def column_shift(values, step_size, lattice_side, column):
    if step_size == 0:
        return values
    inside = (column - step_size >= 0) & (column - step_size < lattice_side)
    wrapped = step_size - lattice_side if step_size > 0 else step_size + lattice_side
    return jnp.where(inside, jnp.roll(values, step_size, axis=2), jnp.roll(values, wrapped, axis=2))


def on_device(
    out_cot,
    mix_weight,
    corr_kernels,
    momentum,
    spin_up,
    layer_input,
    pre_one,
    pre_two,
    conv_weight,
    dilation,
):
    highest = lax.Precision.HIGHEST
    sample_count = out_cot.shape[0]
    chan_block = out_cot.shape[1]
    site_count = out_cot.shape[2]
    sectors = corr_kernels.shape[1]
    lattice_side = corr_kernels.shape[3]
    slab_cells = layer_input.shape[2]
    own_start = lax.axis_index("chan") * chan_block
    own_rows = lax.dynamic_slice_in_dim(mix_weight, own_start, chan_block, 0)
    input_cot = lax.psum_scatter(
        jnp.einsum("oc,son->csn", own_rows, out_cot, preferred_element_type=jnp.float32),
        "chan",
        scatter_dimension=0,
        tiled=True,
    )
    onehot = (momentum[:, None] == jnp.arange(sectors, dtype=jnp.int32)[None, :]).astype(
        jnp.float32
    )
    picked = jnp.einsum("sk,akci->acsi", onehot, corr_kernels, precision=highest)
    positions = jnp.arange(lattice_side, dtype=jnp.int32)
    circ_table = (
        (positions[None, None, :] - positions[None, :, None]) % lattice_side
        == positions[:, None, None]
    ).astype(jnp.float32)
    circulant = jnp.einsum("acsi,ixy->acsxy", picked, circ_table, precision=highest)
    grid_values = input_cot.reshape(chan_block, sample_count, lattice_side, lattice_side)
    halfway = jnp.einsum("csxX,csxy->csXy", circulant[0], grid_values, precision=highest)
    corr_grad = jnp.einsum("csXy,csyY->scXY", halfway, circulant[1], precision=highest)
    corr_grad = corr_grad.reshape(sample_count, chan_block, site_count).astype(jnp.bfloat16)
    regrouped = lax.all_to_all(corr_grad, "chan", split_axis=2, concat_axis=1, tiled=True)
    spin_gate = jnp.where(spin_up == 1, 1.5, 0.5).astype(jnp.float32)[:, None, :]
    grad_now = (regrouped.astype(jnp.float32) * spin_gate).astype(jnp.bfloat16)
    halo_cells = MAXDIL * SIDE
    column = jnp.arange(slab_cells, dtype=jnp.int32) % lattice_side
    norm_factor = 1.0 / math.sqrt(sample_count * lax.axis_size("samp") * site_count)
    layer_grads = [None] * LAYERS
    input_grad = None
    for conv_level in range(LAYERS - 1, -1, -1):
        slope_base = None
        if conv_level == 0:
            layer_values = layer_input
        else:
            saved_pre = pre_one if conv_level == 1 else pre_two
            slope_base = jnp.tanh(saved_pre.astype(jnp.float32))
            layer_values = slope_base.astype(jnp.bfloat16)
        padded = with_halo(grad_now, (("chan", 2),), halo_cells)
        back_sum = jnp.zeros(grad_now.shape, jnp.float32)
        tap_grads = []
        for row_step in (-1, 0, 1):
            for col_step in (-1, 0, 1):
                tap_index = (row_step + 1) * 3 + col_step + 1
                if row_step == 0 and col_step == 0:
                    combined = grad_now
                else:
                    combined = None
                    for dilate in range(1, MAXDIL + 1):
                        slice_begin = halo_cells - row_step * dilate * lattice_side
                        shifted = column_shift(
                            padded[:, :, slice_begin : slice_begin + slab_cells],
                            col_step * dilate,
                            lattice_side,
                            column,
                        )
                        if combined is None:
                            combined = shifted
                        else:
                            chosen_mask = (dilation[conv_level] == dilate)[None, :, None]
                            combined = jnp.where(chosen_mask, shifted, combined)
                back_sum = back_sum + jnp.einsum(
                    "oc,son->scn",
                    conv_weight[conv_level, tap_index],
                    combined,
                    preferred_element_type=jnp.float32,
                )
                tap_grads.append(
                    jnp.einsum(
                        "son,scn->oc", combined, layer_values, preferred_element_type=jnp.float32
                    )
                    * norm_factor
                )
        local_grad = jnp.stack(tap_grads)
        reduced = lax.psum_scatter(
            local_grad.astype(jnp.bfloat16), "chan", scatter_dimension=1, tiled=True
        )
        layer_grads[conv_level] = lax.psum(reduced, "samp").astype(jnp.float32)
        if conv_level > 0:
            grad_now = (back_sum * (1.0 - slope_base * slope_base)).astype(jnp.bfloat16)
        else:
            input_grad = back_sum.astype(jnp.bfloat16)
    weight_grad = jnp.stack(layer_grads)
    return (input_grad, weight_grad)


def solution(mesh):
    in_specs = (
        P("samp", "chan", None),
        P(),
        P(None, None, "chan", None),
        P("samp"),
        P("samp", "chan"),
        P("samp", None, "chan"),
        P("samp", None, "chan"),
        P("samp", None, "chan"),
        P(),
        P(),
    )
    out_specs = (P("samp", None, "chan"), P(None, None, "chan", None))
    return jax.shard_map(
        on_device, mesh=mesh, in_specs=in_specs, out_specs=out_specs, check_vma=False
    )
```

profile of v0, /device:TPU:0, one launch (start us, length us, event | category | flops | bytes accessed | tf_op | source)
XLA Modules:
  0.0 344.3 jit_solution(6769106226334867354)
XLA Ops:
  7.2 3.8 %convolution_bitcast_fusion = f32[256,1,4096]{2,0,1:T(8,128)} fusion(bf16[1,64,4096]{2,1,0:T(8,128)(2,1)} %param.10, bf16[256,256]{1,0:T(8,128)(2,1)} %param.11, s32[]{:T(128)S(6)} %select_n.3285), kind=kOutput, calls=%fused_computation | convolution fusion | flops 134217728 | bytes 4751364 | tf_op jit(solution)/shard_map/oc,son->csn/dot_general | solution.py:55
  12.7 1.8 fusion.5
  14.5 2.3 slice_bitcast_fusion
  16.8 49.8 %reduce-scatter.5.cloned.1.call-done = f32[64,1,4096]{2,0,1:T(8,128)} async-done(((f32[256,1,4096]{2,0,1:T(8,128)}), f32[64,1,4096]{2,0,1:T(8,128)}) %reduce-scatter.5.cloned.1.call-update) | async-done | bytes 1048592 | tf_op jit(solution)/shard_map/reduce_scatter | solution.py:54
  66.7 2.2 reshape.16731
  68.8 6.2 %fusion.2 = f32[64,64,64]{2,1,0:T(8,128)S(1)} fusion(f32[64,64,64]{2,1,0:T(8,128)S(1)} %reshape.16731, f32[64,64,64]{2,0,1:T(8,128)} %get-tuple-element.25), kind=kOutput, calls=%fused_computation.119 | convolution fusion | flops 201326592 | bytes 3145728 | tf_op jit(solution)/shard_map/csxX,csxy->csXy/dot_general | solution.py:71
  75.0 3.3 fusion.7
  79.2 2.8 copy.42
  82.5 23.6 %reduce.18 = bf16[4096,64]{1,0:T(8,128)(2,1)} reduce(bf16[4096,1,64]{2,1,0:T(2,128)(2,1)S(1)} %bitcast.976, bf16[]{:T(256)} %broadcast.4323), dimensions={1}, to_apply=%bitcast.918.reduce_sub_computation | reduce | bytes 1048578
  106.1 2.7 reshape.16776
  108.7 3.5 %all-to-all-start = ((bf16[4,2,32768]{2,1,0:T(2,128)(2,1)}), bf16[4,2,32768]{2,1,0:T(2,128)(2,1)S(1)}, u32[]{:S(2)}, u32[]{:S(2)}) async-start(bf16[4,2,32768]{2,1,0:T(2,128)(2,1)} %reshape.16776), calls=%async_computation.1 | async-start | bytes 1048576 | tf_op jit(solution)/shard_map/all_to_all | solution.py:74
  114.4 6.1 %all-to-all-done = bf16[4,2,32768]{2,1,0:T(2,128)(2,1)S(1)} async-done(((bf16[4,2,32768]{2,1,0:T(2,128)(2,1)}), bf16[4,2,32768]{2,1,0:T(2,128)(2,1)S(1)}, u32[]{:S(2)}, u32[]{:S(2)}) %all-to-all-start) | async-done | bytes 524320 | tf_op jit(solution)/shard_map/all_to_all | solution.py:74
  121.3 2.3 copy.43
  126.2 1.5 collective-permute-start.1
  127.7 1.9 collective-permute-start
  129.6 4.8 %collective-permute-done = bf16[1,256,256]{1,2,0:T(8,128)(2,1)S(1)} collective-permute-done((bf16[1,256,256]{1,2,0:T(8,128)(2,1)S(1)}, bf16[1,256,256]{1,2,0:T(8,128)(2,1)S(1)}, u32[]{:S(2)}, u32[]{:S(2)}) %collective-permute-start) | collective-permute-done | bytes 131104 | tf_op jit(solution)/shard_map/ppermute | solution.py:20
  137.4 3.0 fusion.252
  142.1 1.2 convolution_add_fusion.23
  143.4 3.0 fusion.256
  146.4 1.2 convolution_add_fusion.22
  147.6 3.0 fusion.260
  150.6 1.2 convolution_add_fusion.21
  151.8 1.3 convolution_add_fusion.20
  153.1 3.0 fusion.264
  156.1 1.2 convolution_add_fusion.19
  157.4 3.0 fusion.268
  160.4 1.2 convolution_add_fusion.18
  161.6 1.2 convolution_add_fusion.17
  162.9 3.0 fusion.272
  165.9 1.2 fusion.14
  168.8 2.0 collective-permute-start.2
  177.7 3.0 fusion.276
  182.4 1.2 convolution_add_fusion.15
  183.7 3.0 fusion.280
  186.7 1.2 convolution_add_fusion.14
  187.9 3.0 fusion.284
  190.9 1.2 convolution_add_fusion.13
  192.2 1.2 convolution_add_fusion.12
  193.4 3.0 fusion.288
  196.4 1.2 convolution_add_fusion.11
  197.6 3.0 fusion.292
  200.7 1.2 convolution_add_fusion.10
  201.9 1.2 convolution_add_fusion.9
  203.1 3.0 fusion.296
  206.2 1.2 fusion.15
  208.5 2.0 collective-permute-start.4
  218.1 3.0 fusion.300
  223.8 3.0 fusion.304
  227.8 3.0 fusion.308
  232.9 3.0 fusion.312
  236.8 3.0 fusion.316
  241.9 3.0 fusion.320
  245.9 1.2 fusion.435
  247.1 1.2 convolution_add_fusion.7
  248.3 1.2 convolution_add_fusion.6
  249.6 1.3 convolution_add_fusion.5
  250.8 1.3 convolution_add_fusion.4
  252.1 1.2 convolution_add_fusion.3
  253.4 1.3 convolution_add_fusion.2
  254.7 20.1 %reduce-scatter.7.cloned.1.call-done = bf16[9,64,256]{2,1,0:T(8,128)(2,1)} async-done(((bf16[9,256,256]{2,1,0:T(8,128)(2,1)}), bf16[9,64,256]{2,1,0:T(8,128)(2,1)}) %reduce-scatter.7.cloned.1.call-update) | async-done | bytes 294928 | tf_op jit(solution)/shard_map/reduce_scatter | solution.py:126
  274.9 1.2 convolution_add_fusion.1
  276.1 1.3 fusion.17
  278.4 56.7 %all-reduce.3.cloned.1.call-done = (bf16[1,9,64,256]{3,2,1,0:T(8,128)(2,1)}, bf16[1,9,64,256]{3,2,1,0:T(8,128)(2,1)}, bf16[1,9,64,256]{3,2,1,0:T(8,128)(2,1)}) async-done(((bf16[1,9,64,256]{3,2,1,0:T(8,128)(2,1)}, bf16[1,9,64,256]{3,2,1,0:T(8,128)(2,1)}, bf16[1,9,64,256]{3,2,1,0:T(8,128)(2,1)}), (bf16[1,9,64,256]{3,2,1,0:T(8,128)(2,1)}, bf16[1,9,64,256]{3,2,1,0:T(8,128)(2,1)}, ...) | async-done | bytes 884752 | tf_op jit(solution)/shard_map/psum | solution.py:129
  335.0 2.5 maximum_convert_fusion
  (210 shorter events, 41.9 us)
Async XLA Ops:
  7.2 4.7 %copy-start = (f32[2,12,64,64]{3,2,1,0:T(8,128)S(1)}, f32[2,12,64,64]{3,2,1,0:T(8,128)}, u32[]{:S(2)}) copy-start(f32[2,12,64,64]{3,2,1,0:T(8,128)} %param.12) | copy-start | bytes 1179652
  7.2 59.5 %reduce-scatter.5.cloned.1.call-start = ((), (), s32[]{:S(2)}) async-start(), calls=%async_computation.5 | async-start | bytes 5242880 | tf_op jit(solution)/shard_map/reduce_scatter | solution.py:54
  68.8 6.2 %copy-start.2 = (f32[64,64,64]{2,0,1:T(8,128)S(1)}, f32[64,64,64]{2,0,1:T(8,128)}, u32[]{:S(2)}) copy-start(f32[64,64,64]{2,0,1:T(8,128)} %get-tuple-element.24) | copy-start | bytes 3145732
  106.1 6.2 %copy-start.15 = (bf16[1,256,1024]{2,1,0:T(8,128)(2,1)S(1)}, bf16[1,256,1024]{2,1,0:T(8,128)(2,1)}, u32[]{:S(2)}) copy-start(bf16[1,256,1024]{2,1,0:T(8,128)(2,1)} %param.16) | copy-start | bytes 1572868
  106.1 7.2 %copy-start.16 = (bf16[1,256,1024]{2,1,0:T(8,128)(2,1)S(1)}, bf16[1,256,1024]{2,1,0:T(8,128)(2,1)}, u32[]{:S(2)}) copy-start(bf16[1,256,1024]{2,1,0:T(8,128)(2,1)} %param.17) | copy-start | bytes 1572868
  106.1 8.2 %copy-start.18 = (s32[3,256]{1,0:T(4,128)S(1)}, s32[3,256]{1,0:T(4,128)}, u32[]{:S(2)}) copy-start(s32[3,256]{1,0:T(4,128)} %param.19) | copy-start | bytes 9220
  106.1 8.3 %copy-start.17 = (s32[1,1024]{1,0:T(1,128)S(1)}, s32[1,1024]{1,0:T(1,128)}, u32[]{:S(2)}) copy-start(s32[1,1024]{1,0:T(1,128)} %param.14) | copy-start | bytes 12292
  108.7 11.7 %all-to-all-start = ((bf16[4,2,32768]{2,1,0:T(2,128)(2,1)}), bf16[4,2,32768]{2,1,0:T(2,128)(2,1)S(1)}, u32[]{:S(2)}, u32[]{:S(2)}) async-start(bf16[4,2,32768]{2,1,0:T(2,128)(2,1)} %reshape.16776), calls=%async_computation.1 | async-start | bytes 1048576 | tf_op jit(solution)/shard_map/all_to_all | solution.py:74
  112.2 142.5 %reduce-scatter.11.cloned.1.call-start = ((), (), s32[]{:S(2)}) async-start(), calls=%async_computation.8 | async-start | bytes 1474560 | tf_op jit(solution)/shard_map/reduce_scatter | solution.py:126
  126.2 8.3 %collective-permute-start.1 = (bf16[1,256,256]{1,2,0:T(8,128)(2,1)S(1)}, bf16[1,256,256]{1,2,0:T(8,128)(2,1)S(1)}, u32[]{:S(2)}, u32[]{:S(2)}) collective-permute-start(bf16[1,256,256]{1,2,0:T(8,128)(2,1)S(1)} %get-tuple-element.324), channel_id=1, source_target_pairs={{0,1},{1,2},{2,3},{3,0},{4,5},{5,6},{6,7},{7,4},{8,9},{9,10},{10,1... | collective-permute-start | bytes 393224 | tf_op jit(solution)/shard_map/ppermute | solution.py:19
  127.7 6.7 %collective-permute-start = (bf16[1,256,256]{1,2,0:T(8,128)(2,1)S(1)}, bf16[1,256,256]{1,2,0:T(8,128)(2,1)S(1)}, u32[]{:S(2)}, u32[]{:S(2)}) collective-permute-start(bf16[1,256,256]{1,2,0:T(8,128)(2,1)S(1)} %get-tuple-element.325), channel_id=1, source_target_pairs={{1,0},{2,1},{3,2},{0,3},{5,4},{6,5},{7,6},{4,7},{9,8},{10,9},{11,1... | collective-permute-start | bytes 393224 | tf_op jit(solution)/shard_map/ppermute | solution.py:20
  162.9 3.0 copy-start.8
  167.7 7.3 %collective-permute-start.3 = (bf16[1,256,256]{1,2,0:T(8,128)(2,1)S(1)}, bf16[1,256,256]{1,2,0:T(8,128)(2,1)S(1)}, u32[]{:S(2)}, u32[]{:S(2)}) collective-permute-start(bf16[1,256,256]{1,2,0:T(8,128)(2,1)S(1)} %get-tuple-element.258), channel_id=1, source_target_pairs={{0,1},{1,2},{2,3},{3,0},{4,5},{5,6},{6,7},{7,4},{8,9},{9,10},{10,1... | collective-permute-start | bytes 393224 | tf_op jit(solution)/shard_map/ppermute | solution.py:19
  168.8 6.1 %collective-permute-start.2 = (bf16[1,256,256]{1,2,0:T(8,128)(2,1)S(1)}, bf16[1,256,256]{1,2,0:T(8,128)(2,1)S(1)}, u32[]{:S(2)}, u32[]{:S(2)}) collective-permute-start(bf16[1,256,256]{1,2,0:T(8,128)(2,1)S(1)} %get-tuple-element.259), channel_id=1, source_target_pairs={{1,0},{2,1},{3,2},{0,3},{5,4},{6,5},{7,6},{4,7},{9,8},{10,9},{11,1... | collective-permute-start | bytes 393224 | tf_op jit(solution)/shard_map/ppermute | solution.py:20
  173.8 1.0 copy-start.13
  174.8 79.9 %reduce-scatter.9.cloned.1.call-start = ((), (), s32[]{:S(2)}) async-start(), calls=%async_computation.7 | async-start | bytes 1474560 | tf_op jit(solution)/shard_map/reduce_scatter | solution.py:126
  203.1 3.0 copy-start.7
  207.6 7.8 %collective-permute-start.5 = (bf16[1,256,256]{1,2,0:T(8,128)(2,1)S(1)}, bf16[1,256,256]{1,2,0:T(8,128)(2,1)S(1)}, u32[]{:S(2)}, u32[]{:S(2)}) collective-permute-start(bf16[1,256,256]{1,2,0:T(8,128)(2,1)S(1)} %get-tuple-element.192), channel_id=1, source_target_pairs={{0,1},{1,2},{2,3},{3,0},{4,5},{5,6},{6,7},{7,4},{8,9},{9,10},{10,1... | collective-permute-start | bytes 393224 | tf_op jit(solution)/shard_map/ppermute | solution.py:19
  208.5 6.8 %collective-permute-start.4 = (bf16[1,256,256]{1,2,0:T(8,128)(2,1)S(1)}, bf16[1,256,256]{1,2,0:T(8,128)(2,1)S(1)}, u32[]{:S(2)}, u32[]{:S(2)}) collective-permute-start(bf16[1,256,256]{1,2,0:T(8,128)(2,1)S(1)} %get-tuple-element.193), channel_id=1, source_target_pairs={{1,0},{2,1},{3,2},{0,3},{5,4},{6,5},{7,6},{4,7},{9,8},{10,9},{11,1... | collective-permute-start | bytes 393224 | tf_op jit(solution)/shard_map/ppermute | solution.py:20
  213.9 1.0 copy-start.14
  215.0 59.8 %reduce-scatter.7.cloned.1.call-start = ((), (), s32[]{:S(2)}) async-start(), calls=%async_computation.6 | async-start | bytes 1474560 | tf_op jit(solution)/shard_map/reduce_scatter | solution.py:126
  218.1 3.0 copy-start.19
  222.7 4.1 %copy-start.11 = (bf16[256,1024]{0,1:T(8,128)(2,1)}, bf16[256,1024]{0,1:T(8,128)(2,1)S(1)}, u32[]{:S(2)}) copy-start(bf16[256,1024]{0,1:T(8,128)(2,1)S(1)} %get-tuple-element.123) | copy-start | bytes 1572868
  222.7 18.2 %copy-start.9 = (bf16[256,1024]{0,1:T(8,128)(2,1)}, bf16[256,1024]{0,1:T(8,128)(2,1)S(1)}, u32[]{:S(2)}) copy-start(bf16[256,1024]{0,1:T(8,128)(2,1)S(1)} %get-tuple-element.122) | copy-start | bytes 1572868
  235.8 4.0 %copy-start.3 = (bf16[256,1024]{0,1:T(8,128)(2,1)}, bf16[256,1024]{0,1:T(8,128)(2,1)S(1)}, u32[]{:S(2)}) copy-start(bf16[256,1024]{0,1:T(8,128)(2,1)S(1)} %fusion.312) | copy-start | bytes 1572868
  239.8 2.0 copy-start.5
  244.8 2.3 copy-start.12
  245.9 89.1 %all-reduce.3.cloned.1.call-start = ((), (), s32[]{:S(2)}) async-start(), calls=%async_computation.9 | async-start | bytes 1769472 | tf_op jit(solution)/shard_map/psum | solution.py:129
  249.6 2.6 copy-start.4
  250.8 2.5 copy-start.6
  253.4 21.5 %copy-start.10 = (bf16[256,1024]{0,1:T(8,128)(2,1)S(1)}, bf16[256,1024]{0,1:T(8,128)(2,1)}, u32[]{:S(2)}) copy-start(bf16[256,1024]{0,1:T(8,128)(2,1)} %copy-done.9) | copy-start | bytes 1572868
  276.1 61.5 %copy-start.1 = (f32[2,12,64,64]{3,2,1,0:T(8,128)S(1)}, f32[2,12,64,64]{3,2,1,0:T(8,128)}, u32[]{:S(2)}) copy-start(f32[2,12,64,64]{3,2,1,0:T(8,128)} %param.12) | copy-start | bytes 1179652
Sparse Core Ops, SparseCore 0:
  11.2 55.3 reduce-scatter.4
  174.9 27.8 reduce-scatter.10
  215.1 28.0 reduce-scatter.8
  246.3 28.5 reduce-scatter.6
  277.4 57.5 all-reduce.2
where the time goes:
time: 348 us; the launch traced here: 344 us
  waiting for transfers between devices  138 us (40%)
  other arithmetic  90.3 us (26%)
  matrix products  64.6 us (19%)
  local copies, waits for them, and re-layouts  22.2 us (6%)
  between operations  16.2 us (5%)
  starting transfers between devices  13.4 us (4%)
    psum x1, waiting for transfers between devices, on_device(): layer_grads[conv_level] = lax.psum(reduced, 'samp').astype(jnp.float32)  56.7 us
    select_n x18, other arithmetic, on_device(): combined = jnp.where(chosen_mask, shifted, combined)  54 us
    reduce_scatter x1, waiting for transfers between devices, on_device(): lax.psum_scatter(jnp.einsum('oc,son->csn', own_rows, out_cot, preferred_e...  49.8 us
    dot_general x27, matrix products, on_device(): jnp.einsum('oc,son->scn', conv_weight[conv_level, tap_index], combined, p...  32.9 us
    unnamed x1, other arithmetic  23.6 us
    reduce_scatter x3, waiting for transfers between devices, on_device(): lax.psum_scatter(local_grad.astype(jnp.bfloat16), 'chan', scatter_dimensi...  20.1 us
    dot_general x27, matrix products, on_device(): jnp.einsum('son,scn->oc', combined, layer_values, preferred_element_type=...  15.7 us
    unnamed x46, local copies, waits for them, and re-layouts  9.22 us
  transfers between devices with their start and end apart: 12, of which 5 were waited for; matrix products, arithmetic and copies ran while one was open for 26% of the time, Pallas kernels for 0%

commit v1 on v0

--- a/solution.py
+++ b/solution.py
@@ -71,7 +71,12 @@
     halfway = jnp.einsum("csxX,csxy->csXy", circulant[0], grid_values, precision=highest)
     corr_grad = jnp.einsum("csXy,csyY->scXY", halfway, circulant[1], precision=highest)
     corr_grad = corr_grad.reshape(sample_count, chan_block, site_count).astype(jnp.bfloat16)
-    regrouped = lax.all_to_all(corr_grad, "chan", split_axis=2, concat_axis=1, tiled=True)
+    regrouped = jnp.concatenate(
+        lax.all_to_all(
+            jnp.stack(jnp.split(corr_grad, lax.axis_size("chan"), axis=2)), "chan", 0, 0
+        ),
+        axis=1,
+    )
     spin_gate = jnp.where(spin_up == 1, 1.5, 0.5).astype(jnp.float32)[:, None, :]
     grad_now = (regrouped.astype(jnp.float32) * spin_gate).astype(jnp.bfloat16)
     halo_cells = MAXDIL * SIDE

time: 348 us -> 328 us (0.943)
  other arithmetic: 90.3 us -> 67.9 us
  matrix products: 64.6 us -> 76.5 us
  local copies, waits for them, and re-layouts: 22.2 us -> 13.4 us
    unnamed x1 -> x0, other arithmetic: 23.6 us -> none
    dot_general x27, matrix products: 15.7 us -> 27.6 us  [on_device(): jnp.einsum('son,scn->oc', combined, layer_values, preferred_element_type=...]
    unnamed x46 -> x91, local copies, waits for them, and re-layouts: 9.22 us -> 2.81 us
  transfers between devices with their start and end apart: 12 -> 12, of which waited for: 5 -> 5; matrix products, arithmetic and copies ran while one was open for 26% -> 32% of each run, Pallas kernels for 0% -> 0%
where the time goes in v1:
time: 328 us; the launch traced here: 324 us
  waiting for transfers between devices  137 us (42%)
  matrix products  76.5 us (23%)
  other arithmetic  67.9 us (21%)
  between operations  16.4 us (5%)
  local copies, waits for them, and re-layouts  13.4 us (4%)
  starting transfers between devices  13.2 us (4%)
    psum x1, waiting for transfers between devices, on_device(): layer_grads[conv_level] = lax.psum(reduced, 'samp').astype(jnp.float32)  56.6 us
    select_n x18, other arithmetic, on_device(): combined = jnp.where(chosen_mask, shifted, combined)  54 us
    reduce_scatter x1, waiting for transfers between devices, on_device(): lax.psum_scatter(jnp.einsum('oc,son->csn', own_rows, out_cot, preferred_e...  49.8 us
    dot_general x27, matrix products, on_device(): jnp.einsum('oc,son->scn', conv_weight[conv_level, tap_index], combined, p...  32.8 us
    dot_general x27, matrix products, on_device(): jnp.einsum('son,scn->oc', combined, layer_values, preferred_element_type=...  27.6 us
    reduce_scatter x3, waiting for transfers between devices, on_device(): lax.psum_scatter(local_grad.astype(jnp.bfloat16), 'chan', scatter_dimensi...  19.2 us
    ppermute x3, starting transfers between devices, with_halo(): after = lax.ppermute(leading, axis, down)  6.68 us
  transfers between devices with their start and end apart: 12, of which 5 were waited for; matrix products, arithmetic and copies ran while one was open for 32% of the time, Pallas kernels for 0%

profile of v1, /device:TPU:0, one launch (start us, length us, event | category | flops | bytes accessed | tf_op | source)
XLA Modules:
  0.0 324.1 jit_solution(8321915427252353210)
XLA Ops:
  7.2 3.9 %convolution_bitcast_fusion = f32[256,1,4096]{2,0,1:T(8,128)} fusion(bf16[1,64,4096]{2,1,0:T(8,128)(2,1)} %param.10, bf16[256,256]{1,0:T(8,128)(2,1)} %param.11, s32[]{:T(128)S(6)} %select_n.3285), kind=kOutput, calls=%fused_computation | convolution fusion | flops 134217728 | bytes 4751364 | tf_op jit(solution)/shard_map/oc,son->csn/dot_general | solution.py:55
  12.8 1.8 fusion.5
  14.6 2.3 slice_bitcast_fusion
  16.9 49.8 %reduce-scatter.5.cloned.1.call-done = f32[64,1,4096]{2,0,1:T(8,128)} async-done(((f32[256,1,4096]{2,0,1:T(8,128)}), f32[64,1,4096]{2,0,1:T(8,128)}) %reduce-scatter.5.cloned.1.call-update) | async-done | bytes 1048592 | tf_op jit(solution)/shard_map/reduce_scatter | solution.py:54
  66.7 2.2 reshape.16728
  68.9 6.2 %fusion.2 = f32[64,64,64]{2,1,0:T(8,128)S(1)} fusion(f32[64,64,64]{2,1,0:T(8,128)S(1)} %reshape.16728, f32[64,64,64]{2,0,1:T(8,128)} %get-tuple-element.21), kind=kOutput, calls=%fused_computation.119 | convolution fusion | flops 201326592 | bytes 3145728 | tf_op jit(solution)/shard_map/csxX,csxy->csXy/dot_general | solution.py:71
  75.0 3.3 %fusion.7 = bf16[64,64,64]{2,1,0:T(8,128)(2,1)S(1)} fusion(f32[64,64,64]{2,1,0:T(8,128)S(1)} %fusion.2, f32[64,64,64]{2,0,1:T(8,128)S(1)} %copy-done.2), kind=kOutput, calls=%fused_computation.124 | convolution fusion | flops 201588736 | bytes 2621440 | tf_op jit(solution)/shard_map/csXy,csyY->scXY/dot_general | solution.py:72
  80.2 3.5 %all-to-all-start = ((bf16[4,1,64,1024]{3,2,1,0:T(8,128)(2,1)}), bf16[4,1,64,1024]{3,2,1,0:T(8,128)(2,1)S(1)}, u32[]{:S(2)}, u32[]{:S(2)}) async-start(bf16[4,1,64,1024]{3,2,1,0:T(8,128)(2,1)} %pad_maximum_fusion), calls=%async_computation.1 | async-start | bytes 1048576 | tf_op jit(solution)/shard_map/all_to_all | solution.py:75
  85.5 6.4 %all-to-all-done = bf16[4,1,64,1024]{3,2,1,0:T(8,128)(2,1)S(1)} async-done(((bf16[4,1,64,1024]{3,2,1,0:T(8,128)(2,1)}), bf16[4,1,64,1024]{3,2,1,0:T(8,128)(2,1)S(1)}, u32[]{:S(2)}, u32[]{:S(2)}) %all-to-all-start) | async-done | bytes 524320 | tf_op jit(solution)/shard_map/all_to_all | solution.py:75
  92.8 1.5 collective-permute-start.1
  94.2 1.9 collective-permute-start
  96.2 4.7 %collective-permute-done = bf16[1,256,256]{1,2,0:T(8,128)(2,1)S(1)} collective-permute-done((bf16[1,256,256]{1,2,0:T(8,128)(2,1)S(1)}, bf16[1,256,256]{1,2,0:T(8,128)(2,1)S(1)}, u32[]{:S(2)}, u32[]{:S(2)}) %collective-permute-start) | collective-permute-done | bytes 131104 | tf_op jit(solution)/shard_map/ppermute | solution.py:20
  103.8 3.0 fusion.251
  106.8 1.2 fusion.454
  108.5 1.2 convolution_add_fusion.23
  109.7 3.0 fusion.255
  112.7 1.2 convolution_add_fusion.22
  113.9 3.0 fusion.259
  117.0 1.2 convolution_add_fusion.21
  118.2 1.3 convolution_add_fusion.20
  119.4 3.0 fusion.263
  122.4 1.2 convolution_add_fusion.19
  123.7 3.0 fusion.267
  126.7 1.2 convolution_add_fusion.18
  127.9 1.2 convolution_add_fusion.17
  129.2 3.0 fusion.271
  132.2 1.3 fusion.14
  134.7 1.0 collective-permute-start.3
  135.7 2.0 collective-permute-start.2
  148.9 3.0 fusion.275
  151.9 1.2 fusion.444
  153.6 1.2 convolution_add_fusion.15
  154.9 3.0 fusion.279
  157.9 1.2 convolution_add_fusion.14
  159.1 3.0 fusion.283
  162.1 1.2 convolution_add_fusion.13
  163.3 1.2 convolution_add_fusion.12
  164.5 3.0 fusion.287
  167.5 1.2 convolution_add_fusion.11
  168.8 3.0 fusion.291
  171.8 1.2 convolution_add_fusion.10
  173.1 1.2 convolution_add_fusion.9
  174.3 3.0 fusion.295
  177.3 1.2 fusion.15
  183.1 2.8 collective-permute-start.4
  188.9 1.0 fusion.74
  198.7 3.0 fusion.299
  204.4 3.0 fusion.303
  208.5 3.0 fusion.307
  213.6 3.0 fusion.311
  217.6 3.0 fusion.315
  222.7 3.0 fusion.319
  226.8 1.2 fusion.434
  228.0 1.2 convolution_add_fusion.7
  229.2 1.2 convolution_add_fusion.6
  230.4 1.3 convolution_add_fusion.5
  231.7 1.3 convolution_add_fusion.4
  233.0 1.2 convolution_add_fusion.3
  234.2 1.3 convolution_add_fusion.2
  235.5 19.1 %reduce-scatter.7.cloned.1.call-done = bf16[9,64,256]{2,1,0:T(8,128)(2,1)} async-done(((bf16[9,256,256]{2,1,0:T(8,128)(2,1)}), bf16[9,64,256]{2,1,0:T(8,128)(2,1)}) %reduce-scatter.7.cloned.1.call-update) | async-done | bytes 294928 | tf_op jit(solution)/shard_map/reduce_scatter | solution.py:131
  254.7 1.2 convolution_add_fusion.1
  255.9 1.3 fusion.17
  258.2 56.6 %all-reduce.3.cloned.1.call-done = (bf16[1,9,64,256]{3,2,1,0:T(8,128)(2,1)}, bf16[1,9,64,256]{3,2,1,0:T(8,128)(2,1)}, bf16[1,9,64,256]{3,2,1,0:T(8,128)(2,1)}) async-done(((bf16[1,9,64,256]{3,2,1,0:T(8,128)(2,1)}, bf16[1,9,64,256]{3,2,1,0:T(8,128)(2,1)}, bf16[1,9,64,256]{3,2,1,0:T(8,128)(2,1)}), (bf16[1,9,64,256]{3,2,1,0:T(8,128)(2,1)}, bf16[1,9,64,256]{3,2,1,0:T(8,128)(2,1)}, ...) | async-done | bytes 884752 | tf_op jit(solution)/shard_map/psum | solution.py:134
  314.8 2.5 maximum_convert_fusion
  (252 shorter events, 48.4 us)
Async XLA Ops:
  7.2 4.7 %copy-start = (f32[2,12,64,64]{3,2,1,0:T(8,128)S(1)}, f32[2,12,64,64]{3,2,1,0:T(8,128)}, u32[]{:S(2)}) copy-start(f32[2,12,64,64]{3,2,1,0:T(8,128)} %param.12) | copy-start | bytes 1179652
  7.2 59.5 %reduce-scatter.5.cloned.1.call-start = ((), (), s32[]{:S(2)}) async-start(), calls=%async_computation.5 | async-start | bytes 5242880 | tf_op jit(solution)/shard_map/reduce_scatter | solution.py:54
  11.8 157.0 %copy-start.18 = (pred[1024]{0:T(1024)(128)(4,1)}, pred[1024]{0:T(1024)(128)(4,1)S(1)}, u32[]{:S(2)}) copy-start(pred[1024]{0:T(1024)(128)(4,1)S(1)} %get-tuple-element.326) | copy-start | bytes 3076
  11.8 157.0 %copy-start.20 = (pred[1024]{0:T(1024)(128)(4,1)}, pred[1024]{0:T(1024)(128)(4,1)S(1)}, u32[]{:S(2)}) copy-start(pred[1024]{0:T(1024)(128)(4,1)S(1)} %get-tuple-element.327) | copy-start | bytes 3076
  68.9 6.2 %copy-start.2 = (f32[64,64,64]{2,0,1:T(8,128)S(1)}, f32[64,64,64]{2,0,1:T(8,128)}, u32[]{:S(2)}) copy-start(f32[64,64,64]{2,0,1:T(8,128)} %get-tuple-element.20) | copy-start | bytes 3145732
  78.4 5.3 %copy-start.12 = (bf16[1,256,1024]{2,1,0:T(8,128)(2,1)S(1)}, bf16[1,256,1024]{2,1,0:T(8,128)(2,1)}, u32[]{:S(2)}) copy-start(bf16[1,256,1024]{2,1,0:T(8,128)(2,1)} %param.16) | copy-start | bytes 1572868
  79.2 4.7 %copy-start.13 = (bf16[1,256,1024]{2,1,0:T(8,128)(2,1)S(1)}, bf16[1,256,1024]{2,1,0:T(8,128)(2,1)}, u32[]{:S(2)}) copy-start(bf16[1,256,1024]{2,1,0:T(8,128)(2,1)} %param.17) | copy-start | bytes 1572868
  79.3 5.7 %copy-start.42 = (s32[3,256]{1,0:T(4,128)S(1)}, s32[3,256]{1,0:T(4,128)}, u32[]{:S(2)}) copy-start(s32[3,256]{1,0:T(4,128)} %param.19) | copy-start | bytes 9220
  79.3 6.2 %copy-start.41 = (s32[1,1024]{1,0:T(1,128)S(1)}, s32[1,1024]{1,0:T(1,128)}, u32[]{:S(2)}) copy-start(s32[1,1024]{1,0:T(1,128)} %param.14) | copy-start | bytes 12292
  80.2 11.7 %all-to-all-start = ((bf16[4,1,64,1024]{3,2,1,0:T(8,128)(2,1)}), bf16[4,1,64,1024]{3,2,1,0:T(8,128)(2,1)S(1)}, u32[]{:S(2)}, u32[]{:S(2)}) async-start(bf16[4,1,64,1024]{3,2,1,0:T(8,128)(2,1)} %pad_maximum_fusion), calls=%async_computation.1 | async-start | bytes 1048576 | tf_op jit(solution)/shard_map/all_to_all | solution.py:75
  83.6 151.9 %reduce-scatter.11.cloned.1.call-start = ((), (), s32[]{:S(2)}) async-start(), calls=%async_computation.8 | async-start | bytes 1474560 | tf_op jit(solution)/shard_map/reduce_scatter | solution.py:131
  83.7 90.6 %copy-start.22 = (pred[1024]{0:T(1024)(128)(4,1)}, pred[1024]{0:T(1024)(128)(4,1)S(1)}, u32[]{:S(2)}) copy-start(pred[1024]{0:T(1024)(128)(4,1)S(1)} %get-tuple-element.330) | copy-start | bytes 3076
  83.7 90.6 %copy-start.24 = (pred[1024]{0:T(1024)(128)(4,1)}, pred[1024]{0:T(1024)(128)(4,1)S(1)}, u32[]{:S(2)}) copy-start(pred[1024]{0:T(1024)(128)(4,1)S(1)} %get-tuple-element.331) | copy-start | bytes 3076
  92.8 8.3 %collective-permute-start.1 = (bf16[1,256,256]{1,2,0:T(8,128)(2,1)S(1)}, bf16[1,256,256]{1,2,0:T(8,128)(2,1)S(1)}, u32[]{:S(2)}, u32[]{:S(2)}) collective-permute-start(bf16[1,256,256]{1,2,0:T(8,128)(2,1)S(1)} %get-tuple-element.320), channel_id=1, source_target_pairs={{0,1},{1,2},{2,3},{3,0},{4,5},{5,6},{6,7},{7,4},{8,9},{9,10},{10,1... | collective-permute-start | bytes 393224 | tf_op jit(solution)/shard_map/ppermute | solution.py:19
  94.2 6.7 %collective-permute-start = (bf16[1,256,256]{1,2,0:T(8,128)(2,1)S(1)}, bf16[1,256,256]{1,2,0:T(8,128)(2,1)S(1)}, u32[]{:S(2)}, u32[]{:S(2)}) collective-permute-start(bf16[1,256,256]{1,2,0:T(8,128)(2,1)S(1)} %get-tuple-element.321), channel_id=1, source_target_pairs={{1,0},{2,1},{3,2},{0,3},{5,4},{6,5},{7,6},{4,7},{9,8},{10,9},{11,1... | collective-permute-start | bytes 393224 | tf_op jit(solution)/shard_map/ppermute | solution.py:20
  129.2 3.0 copy-start.7
  134.7 11.5 %collective-permute-start.3 = (bf16[1,256,256]{1,2,0:T(8,128)(2,1)S(1)}, bf16[1,256,256]{1,2,0:T(8,128)(2,1)S(1)}, u32[]{:S(2)}, u32[]{:S(2)}) collective-permute-start(bf16[1,256,256]{1,2,0:T(8,128)(2,1)S(1)} %get-tuple-element.254), channel_id=1, source_target_pairs={{0,1},{1,2},{2,3},{3,0},{4,5},{5,6},{6,7},{7,4},{8,9},{9,10},{10,1... | collective-permute-start | bytes 393224 | tf_op jit(solution)/shard_map/ppermute | solution.py:19
  135.7 10.3 %collective-permute-start.2 = (bf16[1,256,256]{1,2,0:T(8,128)(2,1)S(1)}, bf16[1,256,256]{1,2,0:T(8,128)(2,1)S(1)}, u32[]{:S(2)}, u32[]{:S(2)}) collective-permute-start(bf16[1,256,256]{1,2,0:T(8,128)(2,1)S(1)} %get-tuple-element.255), channel_id=1, source_target_pairs={{1,0},{2,1},{3,2},{0,3},{5,4},{6,5},{7,6},{4,7},{9,8},{10,9},{11,1... | collective-permute-start | bytes 393224 | tf_op jit(solution)/shard_map/ppermute | solution.py:20
  146.0 89.5 %reduce-scatter.9.cloned.1.call-start = ((), (), s32[]{:S(2)}) async-start(), calls=%async_computation.7 | async-start | bytes 1474560 | tf_op jit(solution)/shard_map/reduce_scatter | solution.py:131
  182.9 12.6 %collective-permute-start.5 = (bf16[1,256,256]{1,2,0:T(8,128)(2,1)S(1)}, bf16[1,256,256]{1,2,0:T(8,128)(2,1)S(1)}, u32[]{:S(2)}, u32[]{:S(2)}) collective-permute-start(bf16[1,256,256]{1,2,0:T(8,128)(2,1)S(1)} %get-tuple-element.188), channel_id=1, source_target_pairs={{0,1},{1,2},{2,3},{3,0},{4,5},{5,6},{6,7},{7,4},{8,9},{9,10},{10,1... | collective-permute-start | bytes 393224 | tf_op jit(solution)/shard_map/ppermute | solution.py:19
  183.1 12.3 %collective-permute-start.4 = (bf16[1,256,256]{1,2,0:T(8,128)(2,1)S(1)}, bf16[1,256,256]{1,2,0:T(8,128)(2,1)S(1)}, u32[]{:S(2)}, u32[]{:S(2)}) collective-permute-start(bf16[1,256,256]{1,2,0:T(8,128)(2,1)S(1)} %get-tuple-element.189), channel_id=1, source_target_pairs={{1,0},{2,1},{3,2},{0,3},{5,4},{6,5},{7,6},{4,7},{9,8},{10,9},{11,1... | collective-permute-start | bytes 393224 | tf_op jit(solution)/shard_map/ppermute | solution.py:20
  195.1 59.6 %reduce-scatter.7.cloned.1.call-start = ((), (), s32[]{:S(2)}) async-start(), calls=%async_computation.6 | async-start | bytes 1474560 | tf_op jit(solution)/shard_map/reduce_scatter | solution.py:131
  198.0 0.7 copy-start.19
  198.0 0.7 copy-start.21
  198.0 0.7 copy-start.26
  198.0 0.7 copy-start.27
  198.0 0.7 copy-start.28
  198.0 0.7 copy-start.35
  198.0 0.7 copy-start.36
  198.0 0.7 copy-start.40
  198.7 3.0 copy-start.43
  201.7 2.6 copy-start.14
  201.7 2.6 copy-start.15
  201.8 2.6 copy-start.16
  201.8 2.6 copy-start.17
  201.8 2.6 copy-start.23
  201.8 2.6 copy-start.25
  203.3 4.2 %copy-start.10 = (bf16[256,1024]{0,1:T(8,128)(2,1)}, bf16[256,1024]{0,1:T(8,128)(2,1)S(1)}, u32[]{:S(2)}) copy-start(bf16[256,1024]{0,1:T(8,128)(2,1)S(1)} %get-tuple-element.119) | copy-start | bytes 1572868
  203.3 18.4 %copy-start.8 = (bf16[256,1024]{0,1:T(8,128)(2,1)}, bf16[256,1024]{0,1:T(8,128)(2,1)S(1)}, u32[]{:S(2)}) copy-start(bf16[256,1024]{0,1:T(8,128)(2,1)S(1)} %get-tuple-element.118) | copy-start | bytes 1572868
  204.4 4.1 %copy-start.33 = (bf16[1,256,1,1,1,1,4]{1,6,5,4,3,2,0:T(4,128)(2,1)S(1)}, bf16[1,256,1,1,1,1,4]{1,6,5,4,3,2,0:T(4,128)(2,1)}, u32[]{:S(2)}) copy-start(bf16[1,256,1,1,1,1,4]{1,6,5,4,3,2,0:T(4,128)(2,1)} %get-tuple-element.166) | copy-start | bytes 6148
  204.4 4.0 %copy-start.34 = (bf16[1,256,1,1,1,1,3]{1,6,5,4,3,2,0:T(4,128)(2,1)S(1)}, bf16[1,256,1,1,1,1,3]{1,6,5,4,3,2,0:T(4,128)(2,1)}, u32[]{:S(2)}) copy-start(bf16[1,256,1,1,1,1,3]{1,6,5,4,3,2,0:T(4,128)(2,1)} %get-tuple-element.154) | copy-start | bytes 4612
  204.4 4.0 %copy-start.39 = (bf16[1,256,1,1,1,1,2]{1,6,5,4,3,2,0:T(2,128)(2,1)S(1)}, bf16[1,256,1,1,1,1,2]{1,6,5,4,3,2,0:T(2,128)(2,1)}, u32[]{:S(2)}) copy-start(bf16[1,256,1,1,1,1,2]{1,6,5,4,3,2,0:T(2,128)(2,1)} %get-tuple-element.142) | copy-start | bytes 3076
  211.5 2.1 copy-start.31
  211.5 2.1 copy-start.32
  211.5 2.1 copy-start.38
  216.6 4.0 %copy-start.3 = (bf16[256,1024]{0,1:T(8,128)(2,1)}, bf16[256,1024]{0,1:T(8,128)(2,1)S(1)}, u32[]{:S(2)}) copy-start(bf16[256,1024]{0,1:T(8,128)(2,1)S(1)} %fusion.311) | copy-start | bytes 1572868
  220.6 2.1 copy-start.5
  220.6 2.0 copy-start.29
  220.7 2.0 copy-start.30
  220.7 2.0 copy-start.37
  225.7 2.3 copy-start.11
  226.7 88.1 %all-reduce.3.cloned.1.call-start = ((), (), s32[]{:S(2)}) async-start(), calls=%async_computation.9 | async-start | bytes 1769472 | tf_op jit(solution)/shard_map/psum | solution.py:134
  230.4 2.6 copy-start.4
  231.7 2.5 copy-start.6
  234.2 20.5 %copy-start.9 = (bf16[256,1024]{0,1:T(8,128)(2,1)S(1)}, bf16[256,1024]{0,1:T(8,128)(2,1)}, u32[]{:S(2)}) copy-start(bf16[256,1024]{0,1:T(8,128)(2,1)} %copy-done.8) | copy-start | bytes 1572868
  255.9 61.4 %copy-start.1 = (f32[2,12,64,64]{3,2,1,0:T(8,128)S(1)}, f32[2,12,64,64]{3,2,1,0:T(8,128)}, u32[]{:S(2)}) copy-start(f32[2,12,64,64]{3,2,1,0:T(8,128)} %param.12) | copy-start | bytes 1179652
Sparse Core Ops, SparseCore 0:
  11.3 55.3 reduce-scatter.4
  146.1 27.8 reduce-scatter.10
  195.2 27.7 reduce-scatter.8
  226.9 27.7 reduce-scatter.6
  257.3 57.5 all-reduce.2
